TPU v7x, 512 devices: a whole 4x4x16 slice. The times are simulated.
512 devices in a mesh: pipe: 16 (over z), expert: 32 (over x, y, core).
Axes of the slice: x: 4, y: 4, z: 16, core: 2. Of those that a mesh axis runs over, the one named last changes fastest.
Arguments:
- state: bfloat16 [16, 256, 7168], P('pipe', 'expert'), may hold values from -6 to 6
- fresh: bfloat16 [1, 256, 7168], P(None, 'expert'), may hold values from -6 to 6
- gain: bfloat16 [16, 7168], P('pipe'), may hold values from 0.099609375 to 1.8984375
- w_up: bfloat16 [16, 7168, 4096], P('pipe', None, 'expert'), may hold values from -0.0625 to 0.0625
- w_down: bfloat16 [16, 4096, 7168], P('pipe', 'expert'), may hold values from -0.1875 to 0.1875
- route_ids: int32 [2, 16, 256, 2], P(None, 'pipe', 'expert'), may hold values from 0 to 3, all different within a row; in each aligned block of 8 rows (0 to 7, 8 to 15, ..., all dimensions but the last counted through in order) at most 8 rows name the same one
- gates: float32 [2, 16, 256, 2], P(None, 'pipe', 'expert'), may hold values from 0.05 to 0.5
Outputs:
- after: bfloat16 [16, 256, 7168], P('pipe', 'expert')
Inputs may be any that keep to these rules, and one draw needn't show every extreme that they name: `route_ids`: each token names 2 different experts. Among the 8 tokens of one device at one step and section (aligned blocks of 8 tokens) no expert is named more than 8 times, a bound that some block reaches.
All inputs are finite; a program needn't handle non-finite values.
Results may differ from a plain program's by a relative error of at most 0.006.
Values may be sent and summed in bfloat16 or wider, within the bound.
No kernel may reach another device: no remote copies, remote signals or barrier semaphores. Data moves between devices by JAX's collectives and lax.ppermute only.
A program may use at most 64 MiB of HBM per device.

v0:
```python
import jax
import jax.numpy as jnp
from jax import lax
from jax.sharding import PartitionSpec as P

EXPERTS = 4
TICKS = 2


def shifted(block, axis, distance):
    devices = range(lax.axis_size(axis))
    route = [(i - distance, i) for i in devices if i - distance in devices]
    return lax.ppermute(block, axis, route)


def rms_scaled(rows_in, gain_row):
    wide = rows_in.astype(jnp.float32)
    square = jnp.mean(wide * wide, axis=-1, keepdims=True)
    return (wide * lax.rsqrt(square + 1e-06) * gain_row.astype(jnp.float32)).astype(jnp.bfloat16)


def slot_numbers(blocks, experts):
    onehot = (blocks[..., None] == jnp.arange(experts, dtype=jnp.int32)).astype(jnp.int32)
    before = jnp.cumsum(onehot, axis=-2) - onehot
    return jnp.sum(before * onehot, axis=-1)


def partial_apply(rows_in, weight_up, weight_down):
    hidden = jax.nn.silu(jnp.dot(rows_in, weight_up, preferred_element_type=jnp.float32)).astype(
        jnp.bfloat16
    )
    return jnp.dot(hidden, weight_down, preferred_element_type=jnp.float32).astype(jnp.bfloat16)


def body(state, fresh, gain, w_up, w_down, route_ids, gates):
    devices_all = lax.axis_size("expert")
    group = devices_all // EXPERTS
    tok_rows = state.shape[1]
    model_width = state.shape[2]
    top_count = route_ids.shape[3]
    capacity = min(tok_rows, (2 * tok_rows * top_count + EXPERTS - 1) // EXPERTS)
    weight_up = w_up[0]
    weight_down = w_down[0]
    gain_row = gain[0]
    section_index = lax.axis_index("pipe")
    current = state[0]
    produced = current
    for step_index in range(TICKS):
        chosen = route_ids[step_index, 0]
        gate_rows = gates[step_index, 0]
        normed = rms_scaled(current, gain_row)
        own_slots = slot_numbers(chosen.reshape(1, -1), EXPERTS).reshape(-1)
        position = chosen.reshape(-1) * capacity + own_slots
        token_of = jnp.arange(tok_rows * top_count, dtype=jnp.int32) // top_count
        slot_source = jnp.zeros((EXPERTS * capacity,), jnp.int32).at[position].set(token_of)
        buffer = normed[slot_source].reshape(EXPERTS, capacity, model_width)
        widened = jnp.repeat(buffer, group, axis=0)
        received = lax.all_to_all(widened, "expert", split_axis=0, concat_axis=0, tiled=True)
        flat_rows = received.reshape(-1, model_width)
        partial_value = partial_apply(flat_rows, weight_up, weight_down).reshape(received.shape)
        returned = lax.all_to_all(partial_value, "expert", split_axis=0, concat_axis=0, tiled=True)
        summed = jnp.sum(
            returned.reshape(EXPERTS, group, capacity, model_width).astype(jnp.float32), axis=1
        )
        picked = summed.reshape(-1, model_width)[position].reshape(tok_rows, top_count, model_width)
        expert_sum = jnp.sum(gate_rows[..., None] * picked, axis=1)
        produced = (current.astype(jnp.float32) + expert_sum).astype(jnp.bfloat16)
        if step_index < TICKS - 1:
            arrived = shifted(produced, "pipe", 1)
            current = jnp.where(section_index == 0, fresh[step_index], arrived)
    return produced[None]


def solution(mesh):
    placed = (
        P("pipe", "expert", None),
        P(None, "expert", None),
        P("pipe", None),
        P("pipe", None, "expert"),
        P("pipe", "expert", None),
        P(None, "pipe", "expert", None),
        P(None, "pipe", "expert", None),
    )
    return jax.shard_map(
        body, mesh=mesh, in_specs=placed, out_specs=P("pipe", "expert", None), check_vma=False
    )
```

profile of v0, /device:TPU:128, one launch (start us, length us, event | category | flops | bytes accessed | tf_op | source)
XLA Modules:
  0.0 243.6 jit_solution(736482418564891711)
XLA Ops:
  0.0 0.8 fusion.47
  1.5 0.6 scatter_custom_fusion
  2.1 0.8 mul.125
  2.9 1.1 fusion.14
  4.0 1.0 fusion.16
  5.0 0.8 gather_fusion
  6.3 52.0 %all_to_all.20 = bf16[32,8,7168]{2,1,0:T(8,128)(2,1)} all-to-all(bf16[32,8,7168]{2,1,0:T(8,128)(2,1)S(1)} %bitcast.85), channel_id=1, replica_groups=mesh['pipe'=16,'expert'=32] {'expert'}, dimensions={0} | all-to-all | bytes 7340032 | tf_op jit(solution)/shard_map/all_to_all | solution.py:58
  58.3 6.6 %fusion = bf16[32,8,7168]{2,1,0:T(8,128)(2,1)} fusion(bf16[1,128,7168]{2,1,0:T(8,128)(2,1)S(1)} %copy-done, bf16[1,7168,128]{2,1,0:T(8,128)(2,1)} %param.10, bf16[32,8,7168]{2,1,0:T(8,128)(2,1)} %all_to_all.20), kind=kOutput, calls=%fused_computation.8 | convolution fusion | flops 941522944 | bytes 11010048 | tf_op jit(solution)/shard_map/dot_general | solution.py:32
  64.9 5.0 %all-to-all-start.1 = ((bf16[32,8,7168]{2,1,0:T(8,128)(2,1)}), bf16[32,8,7168]{2,1,0:T(8,128)(2,1)}, u32[]{:S(2)}, u32[]{:S(2)}) async-start(bf16[32,8,7168]{2,1,0:T(8,128)(2,1)} %fusion), calls=%async_computation.1 | async-start | bytes 7340032 | tf_op jit(solution)/shard_map/all_to_all | solution.py:61
  71.2 45.1 %all-to-all-done.1 = bf16[32,8,7168]{2,1,0:T(8,128)(2,1)} async-done(((bf16[32,8,7168]{2,1,0:T(8,128)(2,1)}), bf16[32,8,7168]{2,1,0:T(8,128)(2,1)}, u32[]{:S(2)}, u32[]{:S(2)}) %all-to-all-start.1) | async-done | bytes 3670048 | tf_op jit(solution)/shard_map/all_to_all | solution.py:61
  116.3 2.7 %convert_reduce_fusion.1 = f32[4,8,7168]{2,1,0:T(8,128)S(1)} fusion(bf16[32,8,7168]{2,1,0:T(8,128)(2,1)} %all-to-all-done.1), kind=kLoop, calls=%fused_computation.11 | loop fusion | flops 3440640 | bytes 4587520 | tf_op jit(solution)/shard_map/reduce_sum | solution.py:62
  119.0 0.7 gather_fusion.1
  120.0 0.6 multiply_reduce_fusion.1
  120.7 3.8 %collective-permute-start = (bf16[8,7168]{1,0:T(8,128)(2,1)S(1)}, bf16[8,7168]{1,0:T(8,128)(2,1)S(1)}, u32[]{:S(2)}, u32[]{:S(2)}) collective-permute-start(bf16[8,7168]{1,0:T(8,128)(2,1)S(1)} %fusion.17), channel_id=1, source_target_pairs={{0,32},{32,64},{64,96},{96,128},{128,160},{160,192},{192,224},{224... | collective-permute-start | bytes 344072 | tf_op jit(solution)/shard_map/ppermute | solution.py:13
  124.6 4.0 %collective-permute-done = bf16[8,7168]{1,0:T(8,128)(2,1)S(1)} collective-permute-done((bf16[8,7168]{1,0:T(8,128)(2,1)S(1)}, bf16[8,7168]{1,0:T(8,128)(2,1)S(1)}, u32[]{:S(2)}, u32[]{:S(2)}) %collective-permute-start) | collective-permute-done | bytes 114720 | tf_op jit(solution)/shard_map/ppermute | solution.py:13
  128.9 0.8 gather_fusion.2
  130.2 50.5 %all_to_all.21 = bf16[32,8,7168]{2,1,0:T(8,128)(2,1)} all-to-all(bf16[32,8,7168]{2,1,0:T(8,128)(2,1)S(1)} %bitcast.86), channel_id=1, replica_groups=mesh['pipe'=16,'expert'=32] {'expert'}, dimensions={0} | all-to-all | bytes 7340032 | tf_op jit(solution)/shard_map/all_to_all | solution.py:58
  180.7 6.6 %fusion.1 = bf16[32,8,7168]{2,1,0:T(8,128)(2,1)} fusion(bf16[1,128,7168]{2,1,0:T(8,128)(2,1)S(1)} %copy-done, bf16[1,7168,128]{2,1,0:T(8,128)(2,1)} %param.10, bf16[32,8,7168]{2,1,0:T(8,128)(2,1)} %all_to_all.21), kind=kOutput, calls=%fused_computation.9 | convolution fusion | flops 941522944 | bytes 11010048 | tf_op jit(solution)/shard_map/dot_general | solution.py:32
  187.3 4.8 %all-to-all-start.3 = ((bf16[32,8,7168]{2,1,0:T(8,128)(2,1)}), bf16[32,8,7168]{2,1,0:T(8,128)(2,1)}, u32[]{:S(2)}, u32[]{:S(2)}) async-start(bf16[32,8,7168]{2,1,0:T(8,128)(2,1)} %fusion.1), calls=%async_computation.3 | async-start | bytes 7340032 | tf_op jit(solution)/shard_map/all_to_all | solution.py:61
  192.2 46.4 %all-to-all-done.3 = bf16[32,8,7168]{2,1,0:T(8,128)(2,1)} async-done(((bf16[32,8,7168]{2,1,0:T(8,128)(2,1)}), bf16[32,8,7168]{2,1,0:T(8,128)(2,1)}, u32[]{:S(2)}, u32[]{:S(2)}) %all-to-all-start.3) | async-done | bytes 3670048 | tf_op jit(solution)/shard_map/all_to_all | solution.py:61
  238.6 2.7 %convert_reduce_fusion = f32[4,8,7168]{2,1,0:T(8,128)S(1)} fusion(bf16[32,8,7168]{2,1,0:T(8,128)(2,1)} %all-to-all-done.3), kind=kLoop, calls=%fused_computation.10 | loop fusion | flops 3440640 | bytes 4587520 | tf_op jit(solution)/shard_map/reduce_sum | solution.py:62
  241.3 0.7 gather_fusion.3
  242.2 0.6 multiply_reduce_fusion
  242.9 0.7 fusion.34
  (44 shorter events, 3.8 us)
Async XLA Ops:
  0.0 58.3 %copy-start = (bf16[1,128,7168]{2,1,0:T(8,128)(2,1)S(1)}, bf16[1,128,7168]{2,1,0:T(8,128)(2,1)}, u32[]{:S(2)}) copy-start(bf16[1,128,7168]{2,1,0:T(8,128)(2,1)} %param.11) | copy-start | bytes 5505028
  64.9 5.0 %copy-start.3 = (f32[2,1,8,2]{2,3,1,0:T(2,128)S(1)}, f32[2,1,8,2]{2,3,1,0:T(2,128)}, u32[]{:S(2)}) copy-start(f32[2,1,8,2]{2,3,1,0:T(2,128)} %param.13) | copy-start | bytes 388
  64.9 51.5 %all-to-all-start.1 = ((bf16[32,8,7168]{2,1,0:T(8,128)(2,1)}), bf16[32,8,7168]{2,1,0:T(8,128)(2,1)}, u32[]{:S(2)}, u32[]{:S(2)}) async-start(bf16[32,8,7168]{2,1,0:T(8,128)(2,1)} %fusion), calls=%async_computation.1 | async-start | bytes 7340032 | tf_op jit(solution)/shard_map/all_to_all | solution.py:61
  119.0 1.6 copy-start.1
  119.0 9.6 %copy-start.2 = (bf16[1,8,7168]{2,1,0:T(8,128)(2,1)S(1)}, bf16[1,8,7168]{2,1,0:T(8,128)(2,1)}, u32[]{:S(2)}) copy-start(bf16[1,8,7168]{2,1,0:T(8,128)(2,1)} %param.8) | copy-start | bytes 344068
  120.7 7.9 %collective-permute-start = (bf16[8,7168]{1,0:T(8,128)(2,1)S(1)}, bf16[8,7168]{1,0:T(8,128)(2,1)S(1)}, u32[]{:S(2)}, u32[]{:S(2)}) collective-permute-start(bf16[8,7168]{1,0:T(8,128)(2,1)S(1)} %fusion.17), channel_id=1, source_target_pairs={{0,32},{32,64},{64,96},{96,128},{128,160},{160,192},{192,224},{224... | collective-permute-start | bytes 344072 | tf_op jit(solution)/shard_map/ppermute | solution.py:13
  187.3 51.3 %all-to-all-start.3 = ((bf16[32,8,7168]{2,1,0:T(8,128)(2,1)}), bf16[32,8,7168]{2,1,0:T(8,128)(2,1)}, u32[]{:S(2)}, u32[]{:S(2)}) async-start(bf16[32,8,7168]{2,1,0:T(8,128)(2,1)} %fusion.1), calls=%async_computation.3 | async-start | bytes 7340032 | tf_op jit(solution)/shard_map/all_to_all | solution.py:61
where the time goes:
time: 244 us
  blocking collectives  103 us (42%)
  waiting for transfers between devices  95.6 us (39%)
  starting transfers between devices  13.6 us (6%)
  matrix products  13.1 us (5%)
  other arithmetic  11.9 us (5%)
  local copies, waits for them, and re-layouts  6.52 us (3%)
    all_to_all x2, blocking collectives, body(): lax.all_to_all(widened, 'expert', split_axis=0, concat_axis=0, tiled=True)  103 us
    all_to_all x2, waiting for transfers between devices, body(): lax.all_to_all(partial_value, 'expert', split_axis=0, concat_axis=0, tile...  91.5 us
    dot_general x2, matrix products, partial_apply(): jnp.dot(hidden, weight_down, preferred_element_type=jnp.float32)  13.1 us
    all_to_all x2, starting transfers between devices, body(): lax.all_to_all(partial_value, 'expert', split_axis=0, concat_axis=0, tile...  9.77 us
    reduce_sum x2, other arithmetic, body(): jnp.sum(returned.reshape(EXPERTS, group, capacity, model_width).astype(jn...  5.35 us
  transfers between devices with their start and end apart: 3, of which 3 were waited for; matrix products, arithmetic and copies ran while one was open for 1% of the time, Pallas kernels for 0%

commit v1 on v0

v1 whole, which is shorter than its diff:
```python
import jax
import jax.numpy as jnp
from jax import lax
from jax.experimental import pallas as pl
from jax.experimental.pallas import tpu as pltpu
from jax.sharding import Mesh, PartitionSpec as P

EXPERTS = 4
TICKS = 2
CORES = 2
STAGGER = 15000
TILE = 1024
VMEM = pl.BlockSpec(memory_space=pltpu.VMEM)


def shifted(block, axis, distance):
    devices = range(lax.axis_size(axis))
    route = [(i - distance, i) for i in devices if i - distance in devices]
    return lax.ppermute(block, axis, route)


def swapped(block):
    return lax.ppermute(block, "core", [(i, CORES - 1 - i) for i in range(CORES)])


def rms_scaled(rows_in, gain_row):
    wide = rows_in.astype(jnp.float32)
    square = jnp.mean(wide * wide, axis=-1, keepdims=True)
    return (wide * lax.rsqrt(square + 1e-06) * gain_row.astype(jnp.float32)).astype(jnp.bfloat16)


def exchanged(blocks):
    return lax.all_to_all(blocks, ("plane", "line"), split_axis=0, concat_axis=0, tiled=True)


def first_normed(rows_in, gain_rows, peers):
    def kernel(rows_ref, gain_ref, out_ref):
        normed = rms_scaled(rows_ref[...], gain_ref[...])
        for i in range(peers):
            out_ref[i] = normed

        @pl.when(lax.axis_index("core") != 0)
        def _():
            pl.delay(STAGGER)

    return pl.pallas_call(
        kernel,
        out_shape=jax.ShapeDtypeStruct((peers, *rows_in.shape), jnp.bfloat16),
        in_specs=[VMEM, VMEM],
        out_specs=VMEM,
        compiler_params=pltpu.CompilerParams(vmem_limit_bytes=8 << 20),
    )(rows_in, gain_rows)


def expert_apply(rows_in, up_own, up_other, down_own, down_other):
    count, width = rows_in.shape
    tiles = width // TILE

    def kernel(rows_ref, up_a, up_b, down_a, down_b, out_ref, made, sems):
        def tile(i):
            return pl.ds(i * TILE, TILE)

        raised = 0.0
        for i in range(tiles):
            units = jnp.concatenate([up_a[tile(i), :], up_b[tile(i), :]], axis=1)
            raised = raised + jnp.dot(
                rows_ref[:, tile(i)], units, preferred_element_type=jnp.float32
            )
        hidden = (raised / (1.0 + jnp.exp(-raised))).astype(jnp.bfloat16)
        copies = []
        for i in range(tiles):
            units = jnp.concatenate([down_a[:, tile(i)], down_b[:, tile(i)]], axis=0)
            made[:, tile(i)] = jnp.dot(
                hidden, units, preferred_element_type=jnp.float32
            ).astype(jnp.bfloat16)
            copy = pltpu.make_async_copy(made.at[:, tile(i)], out_ref.at[:, tile(i)], sems.at[i])
            copy.start()
            copies.append(copy)
        for copy in copies:
            copy.wait()

    return pl.pallas_call(
        kernel,
        out_shape=jax.ShapeDtypeStruct((count, width), jnp.bfloat16),
        in_specs=[VMEM] * 5,
        out_specs=pl.BlockSpec(memory_space=pl.ANY),
        scratch_shapes=[
            pltpu.VMEM((count, width), jnp.bfloat16),
            pltpu.SemaphoreType.DMA((tiles,)),
        ],
        compiler_params=pltpu.CompilerParams(vmem_limit_bytes=16 << 20),
        cost_estimate=pl.CostEstimate(
            flops=8 * count * width * up_own.shape[1],
            transcendentals=2 * count * up_own.shape[1],
            bytes_accessed=2 * width * (2 * count + 4 * up_own.shape[1]),
        ),
    )(rows_in, up_own, up_other, down_own, down_other)


def body(state, fresh, gain, w_up, w_down, route_ids, gates):
    lines = lax.axis_size("line")
    peers = lax.axis_size("plane") * lines
    rows = state.shape[1]
    width = state.shape[2]
    section_index = lax.axis_index("pipe")
    weights = (w_up[0], swapped(w_up[0]), w_down[0], swapped(w_down[0]))
    current = state[0]
    for step_index in range(TICKS):
        if step_index == 0:
            sent = first_normed(current, gain, peers)
        else:
            normed = rms_scaled(current, gain[0])
            sent = jnp.broadcast_to(normed[None], (peers, rows, width))
        received = exchanged(sent)
        partial_value = expert_apply(received.reshape(peers * rows, width), *weights)
        returned = exchanged(partial_value.reshape(peers, rows, width))
        chosen = route_ids[step_index, 0][..., None] == jnp.arange(EXPERTS, dtype=jnp.int32)
        weight = jnp.sum(jnp.where(chosen, gates[step_index, 0][..., None], 0.0), axis=1)
        summed = jnp.sum(returned.reshape(EXPERTS, lines, rows, width).astype(jnp.float32), axis=1)
        expert_sum = jnp.sum(weight.T[..., None] * summed, axis=0)
        produced = (current.astype(jnp.float32) + expert_sum).astype(jnp.bfloat16)
        if step_index < TICKS - 1:
            arrived = shifted(produced, "pipe", 1)
            current = jnp.where(section_index == 0, fresh[step_index], arrived)
    return produced[None]


def solution(mesh):
    sections, devices = mesh.devices.shape
    lines = devices // (EXPERTS * CORES)
    grid = Mesh(
        mesh.devices.reshape(sections, EXPERTS, lines, CORES), ("pipe", "plane", "line", "core")
    )
    expert = ("plane", "line", "core")
    placed = (
        P("pipe", expert, None),
        P(None, expert, None),
        P("pipe", None),
        P("pipe", None, expert),
        P("pipe", expert, None),
        P(None, "pipe", expert, None),
        P(None, "pipe", expert, None),
    )
    return jax.shard_map(
        body, mesh=grid, in_specs=placed, out_specs=P("pipe", expert, None), check_vma=False
    )
```

time: 244 us -> 123 us (0.50)
  the two profiles are of different devices: /device:TPU:128 before, /device:TPU:385 now
where the time goes in v1:
time: 123 us; the launch traced here: 122 us
  blocking collectives  56.3 us (46%)
  waiting for transfers between devices  39.1 us (32%)
  starting transfers between devices  15.3 us (12%)
  Pallas kernels  6.15 us (5%)
  other arithmetic  3.43 us (3%)
  local copies, waits for them, and re-layouts  1.88 us (2%)
    all_to_all x2, blocking collectives, exchanged(): lax.all_to_all(blocks, ('plane', 'line'), split_axis=0, concat_axis=0, ti...  56.3 us
    all_to_all x2, waiting for transfers between devices, exchanged(): lax.all_to_all(blocks, ('plane', 'line'), split_axis=0, concat_axis=0, ti...  34.8 us
    all_to_all x2, starting transfers between devices, exchanged(): lax.all_to_all(blocks, ('plane', 'line'), split_axis=0, concat_axis=0, ti...  8.16 us
    pallas_call x2, Pallas kernels, expert_apply(): pl.pallas_call(kernel, out_shape=jax.ShapeDtypeStruct((count, width), jnp...  5.87 us
    ppermute x2, starting transfers between devices, swapped(): lax.ppermute(block, 'core', [(i, CORES - 1 - i) for i in range(CORES)])  4.5 us
    ppermute x1, waiting for transfers between devices, shifted(): return lax.ppermute(block, axis, route)  4.33 us
    ppermute x1, starting transfers between devices, shifted(): return lax.ppermute(block, axis, route)  2.65 us
  transfers between devices with their start and end apart: 5, of which 3 were waited for; matrix products, arithmetic and copies ran while one was open for 0% of the time, Pallas kernels for 0%

profile of v1, /device:TPU:385, one launch (start us, length us, event | category | flops | bytes accessed | tf_op | source)
XLA Modules:
  0.0 122.5 jit_solution(16901342133857120568)
XLA Ops:
  0.0 2.6 %collective-permute-start = (bf16[7168,128]{1,0:T(8,128)(2,1)}, bf16[7168,128]{1,0:T(8,128)(2,1)S(1)}, u32[]{:S(2)}, u32[]{:S(2)}) collective-permute-start(bf16[7168,128]{1,0:T(8,128)(2,1)} %bitcast.32), channel_id=1, source_target_pairs={{0,1},{1,0},{2,3},{3,2},{4,5},{5,4},{6,7},{7,6},{8,9},{9,8},{10,11... | collective-permute-start | bytes 5505032 | tf_op jit(solution)/shard_map/ppermute | solution.py:23
  2.6 1.9 %collective-permute-start.1 = (bf16[128,7168]{1,0:T(8,128)(2,1)}, bf16[128,7168]{1,0:T(8,128)(2,1)S(1)}, u32[]{:S(2)}, u32[]{:S(2)}) collective-permute-start(bf16[128,7168]{1,0:T(8,128)(2,1)} %bitcast.35), channel_id=1, source_target_pairs={{0,1},{1,0},{2,3},{3,2},{4,5},{5,4},{6,7},{7,6},{8,9},{9,8},{10,11... | collective-permute-start | bytes 5505032 | tf_op jit(solution)/shard_map/ppermute | solution.py:23
  4.5 0.0 copy-start.7
  4.5 0.9 copy-done.7
  5.4 0.7 copy-done.9
  6.2 0.3 shard_map.73
  6.5 37.6 %all_to_all.20 = bf16[16,8,7168]{2,1,0:T(8,128)(2,1)S(1)} all-to-all(bf16[16,8,7168]{2,1,0:T(8,128)(2,1)S(1)} %shard_map.73), channel_id=1, replica_groups=mesh['pipe'=16,'plane'=4,'line'=4,'core'=2] {'plane','line'}, dimensions={0} | all-to-all | bytes 3670016 | tf_op jit(solution)/shard_map/all_to_all | solution.py:33
  44.1 3.0 %shard_map.74 = bf16[128,7168]{1,0:T(8,128)(2,1)} custom-call(bf16[128,7168]{1,0:T(8,128)(2,1)S(1)} %bitcast.30, bf16[7168,128]{1,0:T(8,128)(2,1)S(1)} %bitcast.33, bf16[7168,128]{1,0:T(8,128)(2,1)S(1)} %collective-permute-done.up_b, bf16[128,7168]{1,0:T(8,128)(2,1)S(1)} %bitcast.36, bf16[128,7168]{1,0:T(8,128)(2,1)S(1)} %collective-permute-done.1.down_b), custom_call_target="tpu_custom_call" | custom-call | flops 939524096 | bytes 11010048 | tf_op jit(solution)/shard_map/pallas_call | solution.py:82
  47.1 4.4 %all-to-all-start.1 = ((bf16[16,8,7168]{2,1,0:T(8,128)(2,1)}), bf16[16,8,7168]{2,1,0:T(8,128)(2,1)}, u32[]{:S(2)}, u32[]{:S(2)}) async-start(bf16[16,8,7168]{2,1,0:T(8,128)(2,1)} %bitcast.8), calls=%async_computation.1 | async-start | bytes 3670016 | tf_op jit(solution)/shard_map/all_to_all | solution.py:33
  51.6 17.0 %all-to-all-done.1 = bf16[16,8,7168]{2,1,0:T(8,128)(2,1)} async-done(((bf16[16,8,7168]{2,1,0:T(8,128)(2,1)}), bf16[16,8,7168]{2,1,0:T(8,128)(2,1)}, u32[]{:S(2)}, u32[]{:S(2)}) %all-to-all-start.1) | async-done | bytes 1835040 | tf_op jit(solution)/shard_map/all_to_all | solution.py:33
  68.6 1.9 %convert_reduce_fusion.1 = f32[4,8,7168]{2,1,0:T(8,128)S(1)} fusion(bf16[16,8,7168]{2,1,0:T(8,128)(2,1)} %all-to-all-done.1), kind=kLoop, calls=%fused_computation.1 | loop fusion | flops 1605632 | bytes 2752512 | tf_op jit(solution)/shard_map/reduce_sum | solution.py:119
  70.5 0.1 multiply_reduce_fusion.1
  70.7 2.6 %collective-permute-start.2 = (bf16[8,7168]{1,0:T(8,128)(2,1)S(1)}, bf16[8,7168]{1,0:T(8,128)(2,1)S(1)}, u32[]{:S(2)}, u32[]{:S(2)}) collective-permute-start(bf16[8,7168]{1,0:T(8,128)(2,1)S(1)} %add_convert_fusion), channel_id=1, source_target_pairs={{0,32},{32,64},{64,96},{96,128},{128,160},{160,192},{192,224},{224... | collective-permute-start | bytes 344072 | tf_op jit(solution)/shard_map/ppermute | solution.py:19
  73.4 4.3 %collective-permute-done.2 = bf16[8,7168]{1,0:T(8,128)(2,1)S(1)} collective-permute-done((bf16[8,7168]{1,0:T(8,128)(2,1)S(1)}, bf16[8,7168]{1,0:T(8,128)(2,1)S(1)}, u32[]{:S(2)}, u32[]{:S(2)}) %collective-permute-start.2) | collective-permute-done | bytes 114720 | tf_op jit(solution)/shard_map/ppermute | solution.py:19
  77.7 0.2 fusion
  77.9 0.1 fusion.2
  78.0 0.2 broadcast_in_dim.42
  78.2 18.7 %all_to_all.21 = bf16[16,8,7168]{2,1,0:T(8,128)(2,1)S(1)} all-to-all(bf16[16,8,7168]{2,1,0:T(8,128)(2,1)S(1)} %broadcast_in_dim.42), channel_id=1, replica_groups=mesh['pipe'=16,'plane'=4,'line'=4,'core'=2] {'plane','line'}, dimensions={0} | all-to-all | bytes 3670016 | tf_op jit(solution)/shard_map/all_to_all | solution.py:33
  96.9 2.9 %shard_map.75 = bf16[128,7168]{1,0:T(8,128)(2,1)} custom-call(bf16[128,7168]{1,0:T(8,128)(2,1)S(1)} %bitcast.31, bf16[7168,128]{1,0:T(8,128)(2,1)S(1)} %bitcast.34, bf16[7168,128]{1,0:T(8,128)(2,1)S(1)} %copy-done.4, bf16[128,7168]{1,0:T(8,128)(2,1)S(1)} %bitcast.37, bf16[128,7168]{1,0:T(8,128)(2,1)S(1)} %copy-done.6), custom_call_target="tpu_custom_call" | custom-call | flops 939524096 | bytes 11010048 | tf_op jit(solution)/shard_map/pallas_call | solution.py:82
  99.9 3.7 %all-to-all-start.3 = ((bf16[16,8,7168]{2,1,0:T(8,128)(2,1)}), bf16[16,8,7168]{2,1,0:T(8,128)(2,1)S(1)}, u32[]{:S(2)}, u32[]{:S(2)}) async-start(bf16[16,8,7168]{2,1,0:T(8,128)(2,1)} %bitcast.15), calls=%async_computation.3 | async-start | bytes 3670016 | tf_op jit(solution)/shard_map/all_to_all | solution.py:33
  103.6 17.8 %all-to-all-done.3 = bf16[16,8,7168]{2,1,0:T(8,128)(2,1)S(1)} async-done(((bf16[16,8,7168]{2,1,0:T(8,128)(2,1)}), bf16[16,8,7168]{2,1,0:T(8,128)(2,1)S(1)}, u32[]{:S(2)}, u32[]{:S(2)}) %all-to-all-start.3) | async-done | bytes 1835040 | tf_op jit(solution)/shard_map/all_to_all | solution.py:33
  121.4 0.3 convert_reduce_fusion
  121.7 0.1 multiply_reduce_fusion
  121.8 0.7 fusion.4
  (34 shorter events, 0.2 us)
Async XLA Ops:
  0.0 44.1 %collective-permute-start = (bf16[7168,128]{1,0:T(8,128)(2,1)}, bf16[7168,128]{1,0:T(8,128)(2,1)S(1)}, u32[]{:S(2)}, u32[]{:S(2)}) collective-permute-start(bf16[7168,128]{1,0:T(8,128)(2,1)} %bitcast.32), channel_id=1, source_target_pairs={{0,1},{1,0},{2,3},{3,2},{4,5},{5,4},{6,7},{7,6},{8,9},{9,8},{10,11... | collective-permute-start | bytes 5505032 | tf_op jit(solution)/shard_map/ppermute | solution.py:23
  2.6 41.5 %collective-permute-start.1 = (bf16[128,7168]{1,0:T(8,128)(2,1)}, bf16[128,7168]{1,0:T(8,128)(2,1)S(1)}, u32[]{:S(2)}, u32[]{:S(2)}) collective-permute-start(bf16[128,7168]{1,0:T(8,128)(2,1)} %bitcast.35), channel_id=1, source_target_pairs={{0,1},{1,0},{2,3},{3,2},{4,5},{5,4},{6,7},{7,6},{8,9},{9,8},{10,11... | collective-permute-start | bytes 5505032 | tf_op jit(solution)/shard_map/ppermute | solution.py:23
  4.5 0.9 copy-start.7
  5.4 0.7 copy-start.9
  6.4 37.6 %copy-start = (bf16[1,7168,128]{2,1,0:T(8,128)(2,1)S(1)}, bf16[1,7168,128]{2,1,0:T(8,128)(2,1)}, u32[]{:S(2)}) copy-start(bf16[1,7168,128]{2,1,0:T(8,128)(2,1)} %param.10) | copy-start | bytes 5505028
  6.5 37.6 %copy-start.1 = (bf16[1,128,7168]{2,1,0:T(8,128)(2,1)S(1)}, bf16[1,128,7168]{2,1,0:T(8,128)(2,1)}, u32[]{:S(2)}) copy-start(bf16[1,128,7168]{2,1,0:T(8,128)(2,1)} %param.11) | copy-start | bytes 5505028
  44.1 3.0 %copy-start.3 = (bf16[7168,128]{1,0:T(8,128)(2,1)}, bf16[7168,128]{1,0:T(8,128)(2,1)S(1)}, u32[]{:S(2)}) copy-start(bf16[7168,128]{1,0:T(8,128)(2,1)S(1)} %collective-permute-done.up_b) | copy-start | bytes 5505028
  44.1 3.0 %copy-start.5 = (bf16[128,7168]{1,0:T(8,128)(2,1)}, bf16[128,7168]{1,0:T(8,128)(2,1)S(1)}, u32[]{:S(2)}) copy-start(bf16[128,7168]{1,0:T(8,128)(2,1)S(1)} %collective-permute-done.1.down_b) | copy-start | bytes 5505028
  47.1 4.5 %copy-start.12 = (s32[2,1,8,2]{2,3,1,0:T(2,128)S(1)}, s32[2,1,8,2]{2,3,1,0:T(2,128)}, u32[]{:S(2)}) copy-start(s32[2,1,8,2]{2,3,1,0:T(2,128)} %param.12) | copy-start | bytes 388
  47.1 4.5 %copy-start.13 = (f32[2,1,8,2]{2,3,1,0:T(2,128)S(1)}, f32[2,1,8,2]{2,3,1,0:T(2,128)}, u32[]{:S(2)}) copy-start(f32[2,1,8,2]{2,3,1,0:T(2,128)} %param.13) | copy-start | bytes 388
  47.1 21.5 %all-to-all-start.1 = ((bf16[16,8,7168]{2,1,0:T(8,128)(2,1)}), bf16[16,8,7168]{2,1,0:T(8,128)(2,1)}, u32[]{:S(2)}, u32[]{:S(2)}) async-start(bf16[16,8,7168]{2,1,0:T(8,128)(2,1)} %bitcast.8), calls=%async_computation.1 | async-start | bytes 3670016 | tf_op jit(solution)/shard_map/all_to_all | solution.py:33
  51.6 19.1 %copy-start.8 = (bf16[1,8,7168]{2,1,0:T(8,128)(2,1)S(1)}, bf16[1,8,7168]{2,1,0:T(8,128)(2,1)}, u32[]{:S(2)}) copy-start(bf16[1,8,7168]{2,1,0:T(8,128)(2,1)} %param.7) | copy-start | bytes 344068
  51.6 21.7 %copy-start.10 = (bf16[1,7168]{1,0:T(2,128)(2,1)S(1)}, bf16[1,7168]{1,0:T(2,128)(2,1)}, u32[]{:S(2)}) copy-start(bf16[1,7168]{1,0:T(2,128)(2,1)} %gain_ref.1) | copy-start | bytes 43012
  51.6 26.1 %copy-start.11 = (bf16[1,8,7168]{2,1,0:T(8,128)(2,1)S(1)}, bf16[1,8,7168]{2,1,0:T(8,128)(2,1)}, u32[]{:S(2)}) copy-start(bf16[1,8,7168]{2,1,0:T(8,128)(2,1)} %param.8) | copy-start | bytes 344068
  70.7 7.0 %collective-permute-start.2 = (bf16[8,7168]{1,0:T(8,128)(2,1)S(1)}, bf16[8,7168]{1,0:T(8,128)(2,1)S(1)}, u32[]{:S(2)}, u32[]{:S(2)}) collective-permute-start(bf16[8,7168]{1,0:T(8,128)(2,1)S(1)} %add_convert_fusion), channel_id=1, source_target_pairs={{0,32},{32,64},{64,96},{96,128},{128,160},{160,192},{192,224},{224... | collective-permute-start | bytes 344072 | tf_op jit(solution)/shard_map/ppermute | solution.py:19
  78.0 18.9 %copy-start.6 = (bf16[128,7168]{1,0:T(8,128)(2,1)S(1)}, bf16[128,7168]{1,0:T(8,128)(2,1)}, u32[]{:S(2)}) copy-start(bf16[128,7168]{1,0:T(8,128)(2,1)} %copy-done.5) | copy-start | bytes 5505028
  78.2 18.7 %copy-start.2 = (bf16[1,128,7168]{2,1,0:T(8,128)(2,1)S(1)}, bf16[1,128,7168]{2,1,0:T(8,128)(2,1)}, u32[]{:S(2)}) copy-start(bf16[1,128,7168]{2,1,0:T(8,128)(2,1)} %param.11) | copy-start | bytes 5505028
  78.2 18.7 %copy-start.4 = (bf16[7168,128]{1,0:T(8,128)(2,1)S(1)}, bf16[7168,128]{1,0:T(8,128)(2,1)}, u32[]{:S(2)}) copy-start(bf16[7168,128]{1,0:T(8,128)(2,1)} %copy-done.3) | copy-start | bytes 5505028
  99.9 21.5 %all-to-all-start.3 = ((bf16[16,8,7168]{2,1,0:T(8,128)(2,1)}), bf16[16,8,7168]{2,1,0:T(8,128)(2,1)S(1)}, u32[]{:S(2)}, u32[]{:S(2)}) async-start(bf16[16,8,7168]{2,1,0:T(8,128)(2,1)} %bitcast.15), calls=%async_computation.3 | async-start | bytes 3670016 | tf_op jit(solution)/shard_map/all_to_all | solution.py:33

commit v2 on v1

v2 whole, which is shorter than its diff:
```python
import jax
import jax.numpy as jnp
from jax import lax
from jax.experimental import pallas as pl
from jax.experimental.pallas import tpu as pltpu
from jax.sharding import Mesh, PartitionSpec as P

EXPERTS = 4
TICKS = 2
CORES = 2
EXPERT_AXES = ("plane", "line", "core")
STAGGER = 12500
TILE = 1024
VMEM = pl.BlockSpec(memory_space=pltpu.VMEM)


def shifted(block, axis, distance):
    devices = range(lax.axis_size(axis))
    route = [(i - distance, i) for i in devices if i - distance in devices]
    return lax.ppermute(block, axis, route)


def swapped(block):
    return lax.ppermute(block, "core", [(i, CORES - 1 - i) for i in range(CORES)])


def rms_scaled(rows_in, gain_row):
    wide = rows_in.astype(jnp.float32)
    square = jnp.mean(wide * wide, axis=-1, keepdims=True)
    return (wide * lax.rsqrt(square + 1e-06) * gain_row.astype(jnp.float32)).astype(jnp.bfloat16)


def leader(plane, line):
    return (plane + line) % CORES


def exchanged(blocks):
    lines = lax.axis_size("line")
    chips = [(plane, line) for plane in range(lax.axis_size("plane")) for line in range(lines)]
    groups = [
        [(plane * lines + line) * CORES + (leader(plane, line) + turn) % CORES for plane, line in chips]
        for turn in range(CORES)
    ]
    return lax.all_to_all(
        blocks, EXPERT_AXES, split_axis=0, concat_axis=0, axis_index_groups=groups, tiled=True
    )


def first_normed(rows_in, gain_rows, peers):
    def kernel(rows_hbm, gain_hbm, out_ref, rows_ref, gain_ref, sems):
        copies = [
            pltpu.make_async_copy(rows_hbm, rows_ref, sems.at[0]),
            pltpu.make_async_copy(gain_hbm, gain_ref, sems.at[1]),
        ]
        for copy in copies:
            copy.start()
        for copy in copies:
            copy.wait()
        normed = rms_scaled(rows_ref[...], gain_ref[...])
        for i in range(peers):
            out_ref[i] = normed

        @pl.when(lax.axis_index("core") != leader(lax.axis_index("plane"), lax.axis_index("line")))
        def _():
            pl.delay(STAGGER)

    return pl.pallas_call(
        kernel,
        out_shape=jax.ShapeDtypeStruct((peers, *rows_in.shape), jnp.bfloat16),
        in_specs=[pl.BlockSpec(memory_space=pl.ANY)] * 2,
        out_specs=VMEM,
        scratch_shapes=[
            pltpu.VMEM(rows_in.shape, jnp.bfloat16),
            pltpu.VMEM(gain_rows.shape, jnp.bfloat16),
            pltpu.SemaphoreType.DMA((2,)),
        ],
        compiler_params=pltpu.CompilerParams(vmem_limit_bytes=8 << 20),
    )(rows_in, gain_rows)


def expert_apply(rows_in, up_own, up_other, down_own, down_other):
    count, width = rows_in.shape
    tiles = width // TILE

    def kernel(rows_ref, up_a, up_b, down_a, down_b, out_ref):
        def tile(i):
            return pl.ds(i * TILE, TILE)

        raised = 0.0
        for i in range(tiles):
            units = jnp.concatenate([up_a[tile(i), :], up_b[tile(i), :]], axis=1)
            raised = raised + jnp.dot(
                rows_ref[:, tile(i)], units, preferred_element_type=jnp.float32
            )
        hidden = (raised / (1.0 + jnp.exp(-raised))).astype(jnp.bfloat16)
        for i in range(tiles):
            units = jnp.concatenate([down_a[:, tile(i)], down_b[:, tile(i)]], axis=0)
            out_ref[:, tile(i)] = jnp.dot(
                hidden, units, preferred_element_type=jnp.float32
            ).astype(jnp.bfloat16)

    return pl.pallas_call(
        kernel,
        out_shape=jax.ShapeDtypeStruct((count, width), jnp.bfloat16),
        in_specs=[VMEM] * 5,
        out_specs=VMEM,
        compiler_params=pltpu.CompilerParams(vmem_limit_bytes=16 << 20),
        cost_estimate=pl.CostEstimate(
            flops=8 * count * width * up_own.shape[1],
            transcendentals=2 * count * up_own.shape[1],
            bytes_accessed=2 * width * (2 * count + 4 * up_own.shape[1]),
        ),
    )(rows_in, up_own, up_other, down_own, down_other)


def body(state, fresh, gain, w_up, w_down, route_ids, gates):
    lines = lax.axis_size("line")
    peers = lax.axis_size("plane") * lines
    rows = state.shape[1]
    width = state.shape[2]
    section_index = lax.axis_index("pipe")
    weights = (w_up[0], swapped(w_up[0]), w_down[0], swapped(w_down[0]))
    chosen = route_ids[:, 0, ..., None] == jnp.arange(EXPERTS, dtype=jnp.int32)
    weights_home = jnp.sum(jnp.where(chosen, gates[:, 0, ..., None], 0.0), axis=2)
    weights_home = [weights_home[step_index].T for step_index in range(TICKS)]
    current = state[0]
    for step_index in range(TICKS):
        if step_index == 0:
            sent = first_normed(current, gain, peers)
            sent, weights_home = lax.optimization_barrier((sent, weights_home))
        else:
            normed = rms_scaled(current, gain[0])
            sent = jnp.broadcast_to(normed[None], (peers, rows, width))
        received = exchanged(sent)
        partial_value = expert_apply(received.reshape(peers * rows, width), *weights)
        returned = exchanged(partial_value.reshape(peers, rows, width))
        summed = jnp.sum(returned.reshape(EXPERTS, lines, rows, width).astype(jnp.float32), axis=1)
        expert_sum = jnp.sum(weights_home[step_index][..., None] * summed, axis=0)
        produced = (current.astype(jnp.float32) + expert_sum).astype(jnp.bfloat16)
        if step_index < TICKS - 1:
            arrived = shifted(produced, "pipe", 1)
            current = jnp.where(section_index == 0, fresh[step_index], arrived)
    return produced[None]


def solution(mesh):
    sections, devices = mesh.devices.shape
    lines = devices // (EXPERTS * CORES)
    grid = Mesh(
        mesh.devices.reshape(sections, EXPERTS, lines, CORES), ("pipe", *EXPERT_AXES)
    )
    placed = (
        P("pipe", EXPERT_AXES, None),
        P(None, EXPERT_AXES, None),
        P("pipe", None),
        P("pipe", None, EXPERT_AXES),
        P("pipe", EXPERT_AXES, None),
        P(None, "pipe", EXPERT_AXES, None),
        P(None, "pipe", EXPERT_AXES, None),
    )
    return jax.shard_map(
        body, mesh=grid, in_specs=placed, out_specs=P("pipe", EXPERT_AXES, None), check_vma=False
    )
```

time: 123 us -> 118 us (0.959)
  waiting for transfers between devices: 39.1 us -> 4.34 us
  blocking collectives: 56.3 us -> 83.7 us
  Pallas kernels: 6.15 us -> 17.2 us
  starting transfers between devices: 15.3 us -> 7.14 us
    all_to_all x2 -> x0, waiting for transfers between devices: 34.8 us -> none  [exchanged(): lax.all_to_all(blocks, ('plane', 'line'), split_axis=0, concat_axis=0, ti...]
    all_to_all x2 -> x4, blocking collectives: 56.3 us -> 83.7 us  [exchanged(): lax.all_to_all(blocks, EXPERT_AXES, split_axis=0, concat_axis=0, axis_ind...]
    pallas_call x1, Pallas kernels: 0.28 us -> 12.9 us  [first_normed(): pl.pallas_call(kernel, out_shape=jax.ShapeDtypeStruct((peers, *rows_in.sh...]
    all_to_all x2 -> x0, starting transfers between devices: 8.16 us -> none  [exchanged(): lax.all_to_all(blocks, ('plane', 'line'), split_axis=0, concat_axis=0, ti...]
    reduce_sum x2, other arithmetic: 2.14 us -> 0.55 us  [body(): jnp.sum(returned.reshape(EXPERTS, lines, rows, width).astype(jnp.float32)...]
    pallas_call x2, Pallas kernels: 5.87 us -> 4.3 us  [expert_apply(): pl.pallas_call(kernel, out_shape=jax.ShapeDtypeStruct((count, width), jnp...]
  transfers between devices with their start and end apart: 5 -> 3, of which waited for: 3 -> 1; matrix products, arithmetic and copies ran while one was open for 0% -> 1% of each run, Pallas kernels for 0% -> 11%
where the time goes in v2:
time: 118 us
  blocking collectives  83.7 us (71%)
  Pallas kernels  17.2 us (15%)
  starting transfers between devices  7.14 us (6%)
  waiting for transfers between devices  4.34 us (4%)
  other arithmetic  2.54 us (2%)
  local copies, waits for them, and re-layouts  2.35 us (2%)
    all_to_all x4, blocking collectives, exchanged(): lax.all_to_all(blocks, EXPERT_AXES, split_axis=0, concat_axis=0, axis_ind...  83.7 us
    pallas_call x1, Pallas kernels, first_normed(): pl.pallas_call(kernel, out_shape=jax.ShapeDtypeStruct((peers, *rows_in.sh...  12.9 us
    ppermute x2, starting transfers between devices, swapped(): lax.ppermute(block, 'core', [(i, CORES - 1 - i) for i in range(CORES)])  4.5 us
    ppermute x1, waiting for transfers between devices, shifted(): return lax.ppermute(block, axis, route)  4.33 us
    pallas_call x2, Pallas kernels, expert_apply(): pl.pallas_call(kernel, out_shape=jax.ShapeDtypeStruct((count, width), jnp...  4.3 us
    ppermute x1, starting transfers between devices, shifted(): return lax.ppermute(block, axis, route)  2.65 us
  transfers between devices with their start and end apart: 3, of which 1 were waited for; matrix products, arithmetic and copies ran while one was open for 1% of the time, Pallas kernels for 11%

profile of v2, /device:TPU:385, one launch (start us, length us, event | category | flops | bytes accessed | tf_op | source)
XLA Modules:
  0.0 117.5 jit_solution(14904194664949490869)
XLA Ops:
  0.0 2.6 %collective-permute-start = (bf16[7168,128]{1,0:T(8,128)(2,1)}, bf16[7168,128]{1,0:T(8,128)(2,1)S(1)}, u32[]{:S(2)}, u32[]{:S(2)}) collective-permute-start(bf16[7168,128]{1,0:T(8,128)(2,1)} %bitcast.34), channel_id=1, source_target_pairs={{0,1},{1,0},{2,3},{3,2},{4,5},{5,4},{6,7},{7,6},{8,9},{9,8},{10,11... | collective-permute-start | bytes 5505032 | tf_op jit(solution)/shard_map/ppermute | solution.py:24
  2.6 1.9 %collective-permute-start.1 = (bf16[128,7168]{1,0:T(8,128)(2,1)}, bf16[128,7168]{1,0:T(8,128)(2,1)S(1)}, u32[]{:S(2)}, u32[]{:S(2)}) collective-permute-start(bf16[128,7168]{1,0:T(8,128)(2,1)} %bitcast.37), channel_id=1, source_target_pairs={{0,1},{1,0},{2,3},{3,2},{4,5},{5,4},{6,7},{7,6},{8,9},{9,8},{10,11... | collective-permute-start | bytes 5505032 | tf_op jit(solution)/shard_map/ppermute | solution.py:24
  4.5 0.7 select_reduce_fusion
  5.2 0.9 copy-done.7
  6.1 0.7 copy-done.9
  6.9 12.9 %shard_map.73 = bf16[16,8,7168]{2,1,0:T(8,128)(2,1)S(1)} custom-call(bf16[8,7168]{1,0:T(8,128)(2,1)S(1)} %bitcast.40, bf16[1,7168]{1,0:T(2,128)(2,1)S(1)} %copy-done.9), custom_call_target="tpu_custom_call" | custom-call | tf_op jit(solution)/shard_map/pallas_call | solution.py:67
  19.9 0.0 copy-start.1
  19.9 23.9 %all_to_all.20 = bf16[16,8,7168]{2,1,0:T(8,128)(2,1)S(1)} all-to-all(bf16[16,8,7168]{2,1,0:T(8,128)(2,1)S(1)} %shard_map.73), channel_id=1, replica_groups={{0,3,4,7,9,10,13,14,16,19,20,23,25,26,29,30},{1,2,5,6,8,11,12,15,17,18,..., dimensions={0} | all-to-all | bytes 3670016 | tf_op jit(solution)/shard_map/all_to_all | solution.py:44
  43.8 2.1 %shard_map.74 = bf16[128,7168]{1,0:T(8,128)(2,1)S(1)} custom-call(bf16[128,7168]{1,0:T(8,128)(2,1)S(1)} %bitcast.30, bf16[7168,128]{1,0:T(8,128)(2,1)S(1)} %bitcast.35, bf16[7168,128]{1,0:T(8,128)(2,1)S(1)} %collective-permute-done.up_b, bf16[128,7168]{1,0:T(8,128)(2,1)S(1)} %bitcast.38, bf16[128,7168]{1,0:T(8,128)(2,1)S(1)} %collective-permute-done.1.down_b), custom_call_target="tpu_custom_call" | custom-call | flops 939524096 | bytes 11010048 | tf_op jit(solution)/shard_map/pallas_call | solution.py:102
  46.0 19.3 %all_to_all.21 = bf16[16,8,7168]{2,1,0:T(8,128)(2,1)S(1)} all-to-all(bf16[16,8,7168]{2,1,0:T(8,128)(2,1)S(1)} %bitcast.33), channel_id=1, replica_groups={{0,3,4,7,9,10,13,14,16,19,20,23,25,26,29,30},{1,2,5,6,8,11,12,15,17,18,..., dimensions={0} | all-to-all | bytes 3670016 | tf_op jit(solution)/shard_map/all_to_all | solution.py:44
  65.3 0.3 convert_reduce_fusion.1
  65.6 0.1 multiply_reduce_fusion.1
  65.7 0.5 copy-done.8
  66.3 2.6 %collective-permute-start.2 = (bf16[8,7168]{1,0:T(8,128)(2,1)S(1)}, bf16[8,7168]{1,0:T(8,128)(2,1)S(1)}, u32[]{:S(2)}, u32[]{:S(2)}) collective-permute-start(bf16[8,7168]{1,0:T(8,128)(2,1)S(1)} %add_convert_fusion), channel_id=1, source_target_pairs={{0,32},{32,64},{64,96},{96,128},{128,160},{160,192},{192,224},{224... | collective-permute-start | bytes 344072 | tf_op jit(solution)/shard_map/ppermute | solution.py:20
  69.0 4.3 %collective-permute-done.2 = bf16[8,7168]{1,0:T(8,128)(2,1)S(1)} collective-permute-done((bf16[8,7168]{1,0:T(8,128)(2,1)S(1)}, bf16[8,7168]{1,0:T(8,128)(2,1)S(1)}, u32[]{:S(2)}, u32[]{:S(2)}) %collective-permute-start.2) | collective-permute-done | bytes 114720 | tf_op jit(solution)/shard_map/ppermute | solution.py:20
  73.3 0.2 fusion
  73.5 0.1 fusion.2
  73.6 0.2 broadcast_in_dim.31
  73.8 20.6 %all_to_all.22 = bf16[16,8,7168]{2,1,0:T(8,128)(2,1)S(1)} all-to-all(bf16[16,8,7168]{2,1,0:T(8,128)(2,1)S(1)} %broadcast_in_dim.31), channel_id=1, replica_groups={{0,3,4,7,9,10,13,14,16,19,20,23,25,26,29,30},{1,2,5,6,8,11,12,15,17,18,..., dimensions={0} | all-to-all | bytes 3670016 | tf_op jit(solution)/shard_map/all_to_all | solution.py:44
  94.4 2.1 %shard_map.75 = bf16[128,7168]{1,0:T(8,128)(2,1)S(1)} custom-call(bf16[128,7168]{1,0:T(8,128)(2,1)S(1)} %bitcast.31, bf16[7168,128]{1,0:T(8,128)(2,1)S(1)} %bitcast.36, bf16[7168,128]{1,0:T(8,128)(2,1)S(1)} %copy-done.4, bf16[128,7168]{1,0:T(8,128)(2,1)S(1)} %bitcast.39, bf16[128,7168]{1,0:T(8,128)(2,1)S(1)} %copy-done.6), custom_call_target="tpu_custom_call" | custom-call | flops 939524096 | bytes 11010048 | tf_op jit(solution)/shard_map/pallas_call | solution.py:102
  96.6 19.8 %all_to_all.23 = bf16[16,8,7168]{2,1,0:T(8,128)(2,1)S(1)} all-to-all(bf16[16,8,7168]{2,1,0:T(8,128)(2,1)S(1)} %bitcast.32), channel_id=1, replica_groups={{0,3,4,7,9,10,13,14,16,19,20,23,25,26,29,30},{1,2,5,6,8,11,12,15,17,18,..., dimensions={0} | all-to-all | bytes 3670016 | tf_op jit(solution)/shard_map/all_to_all | solution.py:44
  116.4 0.3 convert_reduce_fusion
  116.7 0.1 multiply_reduce_fusion
  116.9 0.7 fusion.4
  (26 shorter events, 0.1 us)
Async XLA Ops:
  0.0 43.8 %collective-permute-start = (bf16[7168,128]{1,0:T(8,128)(2,1)}, bf16[7168,128]{1,0:T(8,128)(2,1)S(1)}, u32[]{:S(2)}, u32[]{:S(2)}) collective-permute-start(bf16[7168,128]{1,0:T(8,128)(2,1)} %bitcast.34), channel_id=1, source_target_pairs={{0,1},{1,0},{2,3},{3,2},{4,5},{5,4},{6,7},{7,6},{8,9},{9,8},{10,11... | collective-permute-start | bytes 5505032 | tf_op jit(solution)/shard_map/ppermute | solution.py:24
  2.6 41.2 %collective-permute-start.1 = (bf16[128,7168]{1,0:T(8,128)(2,1)}, bf16[128,7168]{1,0:T(8,128)(2,1)S(1)}, u32[]{:S(2)}, u32[]{:S(2)}) collective-permute-start(bf16[128,7168]{1,0:T(8,128)(2,1)} %bitcast.37), channel_id=1, source_target_pairs={{0,1},{1,0},{2,3},{3,2},{4,5},{5,4},{6,7},{7,6},{8,9},{9,8},{10,11... | collective-permute-start | bytes 5505032 | tf_op jit(solution)/shard_map/ppermute | solution.py:24
  5.2 0.9 copy-start.7
  6.1 0.7 copy-start.9
  19.8 23.9 %copy-start = (bf16[1,7168,128]{2,1,0:T(8,128)(2,1)S(1)}, bf16[1,7168,128]{2,1,0:T(8,128)(2,1)}, u32[]{:S(2)}) copy-start(bf16[1,7168,128]{2,1,0:T(8,128)(2,1)} %param.10) | copy-start | bytes 5505028
  19.9 23.9 %copy-start.1 = (bf16[1,128,7168]{2,1,0:T(8,128)(2,1)S(1)}, bf16[1,128,7168]{2,1,0:T(8,128)(2,1)}, u32[]{:S(2)}) copy-start(bf16[1,128,7168]{2,1,0:T(8,128)(2,1)} %param.11) | copy-start | bytes 5505028
  43.8 2.2 %copy-start.3 = (bf16[7168,128]{1,0:T(8,128)(2,1)}, bf16[7168,128]{1,0:T(8,128)(2,1)S(1)}, u32[]{:S(2)}) copy-start(bf16[7168,128]{1,0:T(8,128)(2,1)S(1)} %collective-permute-done.up_b) | copy-start | bytes 5505028
  43.8 2.2 %copy-start.5 = (bf16[128,7168]{1,0:T(8,128)(2,1)}, bf16[128,7168]{1,0:T(8,128)(2,1)S(1)}, u32[]{:S(2)}) copy-start(bf16[128,7168]{1,0:T(8,128)(2,1)S(1)} %collective-permute-done.1.down_b) | copy-start | bytes 5505028
  65.3 0.9 copy-start.8
  65.3 3.6 %copy-start.10 = (bf16[1,7168]{1,0:T(2,128)(2,1)S(1)}, bf16[1,7168]{1,0:T(2,128)(2,1)}, u32[]{:S(2)}) copy-start(bf16[1,7168]{1,0:T(2,128)(2,1)} %gain_hbm.1) | copy-start | bytes 43012
  65.3 8.0 %copy-start.11 = (bf16[1,8,7168]{2,1,0:T(8,128)(2,1)S(1)}, bf16[1,8,7168]{2,1,0:T(8,128)(2,1)}, u32[]{:S(2)}) copy-start(bf16[1,8,7168]{2,1,0:T(8,128)(2,1)} %param.8) | copy-start | bytes 344068
  66.3 7.0 %collective-permute-start.2 = (bf16[8,7168]{1,0:T(8,128)(2,1)S(1)}, bf16[8,7168]{1,0:T(8,128)(2,1)S(1)}, u32[]{:S(2)}, u32[]{:S(2)}) collective-permute-start(bf16[8,7168]{1,0:T(8,128)(2,1)S(1)} %add_convert_fusion), channel_id=1, source_target_pairs={{0,32},{32,64},{64,96},{96,128},{128,160},{160,192},{192,224},{224... | collective-permute-start | bytes 344072 | tf_op jit(solution)/shard_map/ppermute | solution.py:20
  73.6 20.8 %copy-start.6 = (bf16[128,7168]{1,0:T(8,128)(2,1)S(1)}, bf16[128,7168]{1,0:T(8,128)(2,1)}, u32[]{:S(2)}) copy-start(bf16[128,7168]{1,0:T(8,128)(2,1)} %copy-done.5) | copy-start | bytes 5505028
  73.8 20.7 %copy-start.2 = (bf16[1,128,7168]{2,1,0:T(8,128)(2,1)S(1)}, bf16[1,128,7168]{2,1,0:T(8,128)(2,1)}, u32[]{:S(2)}) copy-start(bf16[1,128,7168]{2,1,0:T(8,128)(2,1)} %param.11) | copy-start | bytes 5505028
  73.8 20.6 %copy-start.4 = (bf16[7168,128]{1,0:T(8,128)(2,1)S(1)}, bf16[7168,128]{1,0:T(8,128)(2,1)}, u32[]{:S(2)}) copy-start(bf16[7168,128]{1,0:T(8,128)(2,1)} %copy-done.3) | copy-start | bytes 5505028

commit v3 on v2

--- a/solution.py
+++ b/solution.py
@@ -46,36 +46,51 @@
     )
 
 
-def first_normed(rows_in, gain_rows, peers):
-    def kernel(rows_hbm, gain_hbm, out_ref, rows_ref, gain_ref, sems):
+def opening(rows_in, gain_rows, ids, values, peers):
+    def kernel(rows_hbm, gain_hbm, ids_hbm, values_hbm, sent_ref, kept_ref, *refs):
+        homes, held, sems = refs[:TICKS], refs[TICKS:-1], refs[-1]
+        sources = (rows_hbm, gain_hbm, ids_hbm, values_hbm)
         copies = [
-            pltpu.make_async_copy(rows_hbm, rows_ref, sems.at[0]),
-            pltpu.make_async_copy(gain_hbm, gain_ref, sems.at[1]),
+            pltpu.make_async_copy(source, target, sems.at[i])
+            for i, (source, target) in enumerate(zip(sources, held))
         ]
         for copy in copies:
             copy.start()
         for copy in copies:
             copy.wait()
+        rows_ref, gain_ref, ids_ref, values_ref = held
         normed = rms_scaled(rows_ref[...], gain_ref[...])
+        kept_ref[...] = rows_ref[...]
         for i in range(peers):
-            out_ref[i] = normed
+            sent_ref[i] = normed
+        for step_index, home_ref in enumerate(homes):
+            number = lax.broadcasted_iota(jnp.int32, home_ref.shape, 0)
+            total = jnp.zeros(home_ref.shape, jnp.float32)
+            for k in range(ids_ref.shape[1]):
+                named = ids_ref[step_index, k : k + 1, :] == number
+                total = total + jnp.where(named, values_ref[step_index, k : k + 1, :], 0.0)
+            home_ref[...] = total
 
         @pl.when(lax.axis_index("core") != leader(lax.axis_index("plane"), lax.axis_index("line")))
         def _():
             pl.delay(STAGGER)
 
+    operands = [
+        pltpu.with_memory_space_constraint(each, pltpu.HBM)
+        for each in (rows_in, gain_rows, ids, values)
+    ]
+    sent = jax.ShapeDtypeStruct((peers, *rows_in.shape), jnp.bfloat16)
+    kept = jax.ShapeDtypeStruct(rows_in.shape, jnp.bfloat16)
+    home = jax.ShapeDtypeStruct((EXPERTS, rows_in.shape[0]), jnp.float32)
     return pl.pallas_call(
         kernel,
-        out_shape=jax.ShapeDtypeStruct((peers, *rows_in.shape), jnp.bfloat16),
-        in_specs=[pl.BlockSpec(memory_space=pl.ANY)] * 2,
-        out_specs=VMEM,
-        scratch_shapes=[
-            pltpu.VMEM(rows_in.shape, jnp.bfloat16),
-            pltpu.VMEM(gain_rows.shape, jnp.bfloat16),
-            pltpu.SemaphoreType.DMA((2,)),
-        ],
+        out_shape=[sent, kept] + [home] * TICKS,
+        in_specs=[pl.BlockSpec(memory_space=pl.ANY)] * len(operands),
+        out_specs=[VMEM] * (2 + TICKS),
+        scratch_shapes=[pltpu.VMEM(each.shape, each.dtype) for each in (rows_in, gain_rows, ids, values)]
+        + [pltpu.SemaphoreType.DMA((len(operands),))],
         compiler_params=pltpu.CompilerParams(vmem_limit_bytes=8 << 20),
-    )(rows_in, gain_rows)
+    )(*operands)
 
 
 def expert_apply(rows_in, up_own, up_other, down_own, down_other):
@@ -120,14 +135,11 @@
     width = state.shape[2]
     section_index = lax.axis_index("pipe")
     weights = (w_up[0], swapped(w_up[0]), w_down[0], swapped(w_down[0]))
-    chosen = route_ids[:, 0, ..., None] == jnp.arange(EXPERTS, dtype=jnp.int32)
-    weights_home = jnp.sum(jnp.where(chosen, gates[:, 0, ..., None], 0.0), axis=2)
-    weights_home = [weights_home[step_index].T for step_index in range(TICKS)]
+    ids, values = (each[:, 0].transpose(0, 2, 1) for each in (route_ids, gates))
     current = state[0]
     for step_index in range(TICKS):
         if step_index == 0:
-            sent = first_normed(current, gain, peers)
-            sent, weights_home = lax.optimization_barrier((sent, weights_home))
+            sent, current, *weights_home = opening(current, gain, ids, values, peers)
         else:
             normed = rms_scaled(current, gain[0])
             sent = jnp.broadcast_to(normed[None], (peers, rows, width))

time: 118 us -> 116 us (0.983)
  local copies, waits for them, and re-layouts: 2.35 us -> 0.21 us
    unnamed x24 -> x18, local copies, waits for them, and re-layouts: 2.18 us -> 0.04 us
  transfers between devices with their start and end apart: 3 -> 3, of which waited for: 1 -> 1; matrix products, arithmetic and copies ran while one was open for 1% -> 0% of each run, Pallas kernels for 11% -> 12%
where the time goes in v3:
time: 116 us; the launch traced here: 115 us
  blocking collectives  83.7 us (72%)
  Pallas kernels  18 us (16%)
  starting transfers between devices  7.14 us (6%)
  waiting for transfers between devices  4.34 us (4%)
  other arithmetic  1.83 us (2%)
    all_to_all x4, blocking collectives, exchanged(): lax.all_to_all(blocks, EXPERT_AXES, split_axis=0, concat_axis=0, axis_ind...  83.7 us
    pallas_call x1, Pallas kernels, opening(): pl.pallas_call(kernel, out_shape=[sent, kept] + [home] * TICKS, in_specs=...  13.7 us
    ppermute x2, starting transfers between devices, swapped(): lax.ppermute(block, 'core', [(i, CORES - 1 - i) for i in range(CORES)])  4.5 us
    ppermute x1, waiting for transfers between devices, shifted(): return lax.ppermute(block, axis, route)  4.33 us
    pallas_call x2, Pallas kernels, expert_apply(): pl.pallas_call(kernel, out_shape=jax.ShapeDtypeStruct((count, width), jnp...  4.3 us
    ppermute x1, starting transfers between devices, shifted(): return lax.ppermute(block, axis, route)  2.65 us
  transfers between devices with their start and end apart: 3, of which 1 were waited for; matrix products, arithmetic and copies ran while one was open for 0% of the time, Pallas kernels for 12%

profile of v3, /device:TPU:385, one launch (start us, length us, event | category | flops | bytes accessed | tf_op | source)
XLA Modules:
  0.0 115.5 jit_solution(14454244072724521190)
XLA Ops:
  0.0 2.6 %collective-permute-start = (bf16[7168,128]{1,0:T(8,128)(2,1)}, bf16[7168,128]{1,0:T(8,128)(2,1)S(1)}, u32[]{:S(2)}, u32[]{:S(2)}) collective-permute-start(bf16[7168,128]{1,0:T(8,128)(2,1)} %bitcast.29), channel_id=1, source_target_pairs={{0,1},{1,0},{2,3},{3,2},{4,5},{5,4},{6,7},{7,6},{8,9},{9,8},{10,11... | collective-permute-start | bytes 5505032 | tf_op jit(solution)/shard_map/ppermute | solution.py:24
  2.6 1.9 %collective-permute-start.1 = (bf16[128,7168]{1,0:T(8,128)(2,1)}, bf16[128,7168]{1,0:T(8,128)(2,1)S(1)}, u32[]{:S(2)}, u32[]{:S(2)}) collective-permute-start(bf16[128,7168]{1,0:T(8,128)(2,1)} %bitcast.32), channel_id=1, source_target_pairs={{0,1},{1,0},{2,3},{3,2},{4,5},{5,4},{6,7},{7,6},{8,9},{9,8},{10,11... | collective-permute-start | bytes 5505032 | tf_op jit(solution)/shard_map/ppermute | solution.py:24
  4.5 13.7 %shard_map.73 = (bf16[16,8,7168]{2,1,0:T(8,128)(2,1)S(1)}, bf16[8,7168]{1,0:T(8,128)(2,1)S(1)}, f32[4,8]{1,0:T(4,128)S(1)}, f32[4,8]{1,0:T(4,128)S(1)}) custom-call(bf16[8,7168]{1,0:T(8,128)(2,1)} %bitcast.35, bf16[1,7168]{1,0:T(2,128)(2,1)} %gain_hbm.1, s32[2,2,8]{2,1,0:T(2,128)} %bitcast.37, f32[2,2,8]{2,1,0:T(2,128)} %bitcast.38), custom_call_target="tpu_custom_call" | custom-call | tf_op jit(solution)/shard_map/pallas_call | solution.py:85
  18.2 0.0 copy-start
  18.3 0.0 copy-start.1
  18.3 23.9 %all_to_all.20 = bf16[16,8,7168]{2,1,0:T(8,128)(2,1)S(1)} all-to-all(bf16[16,8,7168]{2,1,0:T(8,128)(2,1)S(1)} %get-tuple-element.11), channel_id=1, replica_groups={{0,3,4,7,9,10,13,14,16,19,20,23,25,26,29,30},{1,2,5,6,8,11,12,15,17,18,..., dimensions={0} | all-to-all | bytes 3670016 | tf_op jit(solution)/shard_map/all_to_all | solution.py:44
  42.2 0.0 collective-permute-done.up_b
  42.2 0.0 collective-permute-done.1.down_b
  42.2 2.1 %shard_map.74 = bf16[128,7168]{1,0:T(8,128)(2,1)S(1)} custom-call(bf16[128,7168]{1,0:T(8,128)(2,1)S(1)} %bitcast.25, bf16[7168,128]{1,0:T(8,128)(2,1)S(1)} %bitcast.30, bf16[7168,128]{1,0:T(8,128)(2,1)S(1)} %collective-permute-done.up_b, bf16[128,7168]{1,0:T(8,128)(2,1)S(1)} %bitcast.33, bf16[128,7168]{1,0:T(8,128)(2,1)S(1)} %collective-permute-done.1.down_b), custom_call_target="tpu_custom_call" | custom-call | flops 939524096 | bytes 11010048 | tf_op jit(solution)/shard_map/pallas_call | solution.py:117
  44.4 19.3 %all_to_all.21 = bf16[16,8,7168]{2,1,0:T(8,128)(2,1)S(1)} all-to-all(bf16[16,8,7168]{2,1,0:T(8,128)(2,1)S(1)} %bitcast.28), channel_id=1, replica_groups={{0,3,4,7,9,10,13,14,16,19,20,23,25,26,29,30},{1,2,5,6,8,11,12,15,17,18,..., dimensions={0} | all-to-all | bytes 3670016 | tf_op jit(solution)/shard_map/all_to_all | solution.py:44
  63.7 0.3 convert_reduce_fusion.1
  64.0 0.1 multiply_reduce_fusion.1
  64.2 2.6 %collective-permute-start.2 = (bf16[8,7168]{1,0:T(8,128)(2,1)S(1)}, bf16[8,7168]{1,0:T(8,128)(2,1)S(1)}, u32[]{:S(2)}, u32[]{:S(2)}) collective-permute-start(bf16[8,7168]{1,0:T(8,128)(2,1)S(1)} %add_convert_fusion), channel_id=1, source_target_pairs={{0,32},{32,64},{64,96},{96,128},{128,160},{160,192},{192,224},{224... | collective-permute-start | bytes 344072 | tf_op jit(solution)/shard_map/ppermute | solution.py:20
  66.9 4.3 %collective-permute-done.2 = bf16[8,7168]{1,0:T(8,128)(2,1)S(1)} collective-permute-done((bf16[8,7168]{1,0:T(8,128)(2,1)S(1)}, bf16[8,7168]{1,0:T(8,128)(2,1)S(1)}, u32[]{:S(2)}, u32[]{:S(2)}) %collective-permute-start.2) | collective-permute-done | bytes 114720 | tf_op jit(solution)/shard_map/ppermute | solution.py:20
  71.2 0.2 fusion
  71.4 0.1 fusion.2
  71.5 0.2 broadcast_in_dim.4
  71.7 0.0 copy-start.2
  71.7 20.6 %all_to_all.22 = bf16[16,8,7168]{2,1,0:T(8,128)(2,1)S(1)} all-to-all(bf16[16,8,7168]{2,1,0:T(8,128)(2,1)S(1)} %broadcast_in_dim.4), channel_id=1, replica_groups={{0,3,4,7,9,10,13,14,16,19,20,23,25,26,29,30},{1,2,5,6,8,11,12,15,17,18,..., dimensions={0} | all-to-all | bytes 3670016 | tf_op jit(solution)/shard_map/all_to_all | solution.py:44
  92.4 2.1 %shard_map.75 = bf16[128,7168]{1,0:T(8,128)(2,1)S(1)} custom-call(bf16[128,7168]{1,0:T(8,128)(2,1)S(1)} %bitcast.26, bf16[7168,128]{1,0:T(8,128)(2,1)S(1)} %bitcast.31, bf16[7168,128]{1,0:T(8,128)(2,1)S(1)} %copy-done.4, bf16[128,7168]{1,0:T(8,128)(2,1)S(1)} %bitcast.34, bf16[128,7168]{1,0:T(8,128)(2,1)S(1)} %copy-done.6), custom_call_target="tpu_custom_call" | custom-call | flops 939524096 | bytes 11010048 | tf_op jit(solution)/shard_map/pallas_call | solution.py:117
  94.5 19.8 %all_to_all.23 = bf16[16,8,7168]{2,1,0:T(8,128)(2,1)S(1)} all-to-all(bf16[16,8,7168]{2,1,0:T(8,128)(2,1)S(1)} %bitcast.27), channel_id=1, replica_groups={{0,3,4,7,9,10,13,14,16,19,20,23,25,26,29,30},{1,2,5,6,8,11,12,15,17,18,..., dimensions={0} | all-to-all | bytes 3670016 | tf_op jit(solution)/shard_map/all_to_all | solution.py:44
  114.4 0.3 convert_reduce_fusion
  114.6 0.1 multiply_reduce_fusion
  114.8 0.7 fusion.4
  (18 shorter events, 0.1 us)
Async XLA Ops:
  0.0 42.2 %collective-permute-start = (bf16[7168,128]{1,0:T(8,128)(2,1)}, bf16[7168,128]{1,0:T(8,128)(2,1)S(1)}, u32[]{:S(2)}, u32[]{:S(2)}) collective-permute-start(bf16[7168,128]{1,0:T(8,128)(2,1)} %bitcast.29), channel_id=1, source_target_pairs={{0,1},{1,0},{2,3},{3,2},{4,5},{5,4},{6,7},{7,6},{8,9},{9,8},{10,11... | collective-permute-start | bytes 5505032 | tf_op jit(solution)/shard_map/ppermute | solution.py:24
  2.6 39.6 %collective-permute-start.1 = (bf16[128,7168]{1,0:T(8,128)(2,1)}, bf16[128,7168]{1,0:T(8,128)(2,1)S(1)}, u32[]{:S(2)}, u32[]{:S(2)}) collective-permute-start(bf16[128,7168]{1,0:T(8,128)(2,1)} %bitcast.32), channel_id=1, source_target_pairs={{0,1},{1,0},{2,3},{3,2},{4,5},{5,4},{6,7},{7,6},{8,9},{9,8},{10,11... | collective-permute-start | bytes 5505032 | tf_op jit(solution)/shard_map/ppermute | solution.py:24
  18.2 23.9 %copy-start = (bf16[1,7168,128]{2,1,0:T(8,128)(2,1)S(1)}, bf16[1,7168,128]{2,1,0:T(8,128)(2,1)}, u32[]{:S(2)}) copy-start(bf16[1,7168,128]{2,1,0:T(8,128)(2,1)} %param.10) | copy-start | bytes 5505028
  18.3 23.9 %copy-start.1 = (bf16[1,128,7168]{2,1,0:T(8,128)(2,1)S(1)}, bf16[1,128,7168]{2,1,0:T(8,128)(2,1)}, u32[]{:S(2)}) copy-start(bf16[1,128,7168]{2,1,0:T(8,128)(2,1)} %param.11) | copy-start | bytes 5505028
  42.2 2.2 %copy-start.3 = (bf16[7168,128]{1,0:T(8,128)(2,1)}, bf16[7168,128]{1,0:T(8,128)(2,1)S(1)}, u32[]{:S(2)}) copy-start(bf16[7168,128]{1,0:T(8,128)(2,1)S(1)} %collective-permute-done.up_b) | copy-start | bytes 5505028
  42.2 2.2 %copy-start.5 = (bf16[128,7168]{1,0:T(8,128)(2,1)}, bf16[128,7168]{1,0:T(8,128)(2,1)S(1)}, u32[]{:S(2)}) copy-start(bf16[128,7168]{1,0:T(8,128)(2,1)S(1)} %collective-permute-done.1.down_b) | copy-start | bytes 5505028
  63.7 3.1 %copy-start.7 = (bf16[1,7168]{1,0:T(2,128)(2,1)S(1)}, bf16[1,7168]{1,0:T(2,128)(2,1)}, u32[]{:S(2)}) copy-start(bf16[1,7168]{1,0:T(2,128)(2,1)} %gain_hbm.1) | copy-start | bytes 43012
  63.7 7.5 %copy-start.8 = (bf16[1,8,7168]{2,1,0:T(8,128)(2,1)S(1)}, bf16[1,8,7168]{2,1,0:T(8,128)(2,1)}, u32[]{:S(2)}) copy-start(bf16[1,8,7168]{2,1,0:T(8,128)(2,1)} %param.8) | copy-start | bytes 344068
  64.2 7.0 %collective-permute-start.2 = (bf16[8,7168]{1,0:T(8,128)(2,1)S(1)}, bf16[8,7168]{1,0:T(8,128)(2,1)S(1)}, u32[]{:S(2)}, u32[]{:S(2)}) collective-permute-start(bf16[8,7168]{1,0:T(8,128)(2,1)S(1)} %add_convert_fusion), channel_id=1, source_target_pairs={{0,32},{32,64},{64,96},{96,128},{128,160},{160,192},{192,224},{224... | collective-permute-start | bytes 344072 | tf_op jit(solution)/shard_map/ppermute | solution.py:20
  71.5 20.8 %copy-start.6 = (bf16[128,7168]{1,0:T(8,128)(2,1)S(1)}, bf16[128,7168]{1,0:T(8,128)(2,1)}, u32[]{:S(2)}) copy-start(bf16[128,7168]{1,0:T(8,128)(2,1)} %copy-done.5) | copy-start | bytes 5505028
  71.7 20.7 %copy-start.2 = (bf16[1,128,7168]{2,1,0:T(8,128)(2,1)S(1)}, bf16[1,128,7168]{2,1,0:T(8,128)(2,1)}, u32[]{:S(2)}) copy-start(bf16[1,128,7168]{2,1,0:T(8,128)(2,1)} %param.11) | copy-start | bytes 5505028
  71.7 20.6 %copy-start.4 = (bf16[7168,128]{1,0:T(8,128)(2,1)S(1)}, bf16[7168,128]{1,0:T(8,128)(2,1)}, u32[]{:S(2)}) copy-start(bf16[7168,128]{1,0:T(8,128)(2,1)} %copy-done.3) | copy-start | bytes 5505028
